TPU v7x, 32 devices: a whole 2x2x4 slice. The times are simulated.
32 devices in a mesh: grp: 4 (over y, x), dp: 8 (over z, core).
Axes of the slice: x: 2, y: 2, z: 4, core: 2. Of those that a mesh axis runs over, the one named last changes fastest.
Arguments:
- hidden: bfloat16 [16384, 768], P(('grp', 'dp')), may hold values from -6 to 6
- weight: bfloat16 [768, 2048], P('dp'), may hold values from -1 to 1
- target: bfloat16 [16384, 2048], P(('grp', 'dp')), may hold values from -6 to 6
Outputs:
- hidden_grad: bfloat16 [16384, 768], P(('grp', 'dp'))
- combined: float32 [768, 2048], P('dp', 'grp')
All inputs are finite; a program needn't handle non-finite values.
Results may differ from a plain program's by a relative error of at most 0.008.
Values may be sent and summed in bfloat16 or wider, within the bound.
A program may use at most 64 MiB of HBM per device.

v0:
```python
import math

import jax
import jax.numpy as jnp
from jax import lax
from jax.sharding import PartitionSpec as P


def partner(value, axis, stride):
    mask = 2**stride
    pairs = [(source, source ^ mask) for source in range(lax.axis_size(axis))]
    return lax.ppermute(value, axis, pairs)


def coefficients(own_sq, other_sq, cross):
    eps = 1e-06
    return (1.0 - cross / (2.0 * (own_sq + eps)), 1.0 - cross / (2.0 * (other_sq + eps)))


def shards(hidden, weight, target):
    rows = hidden.shape[0]
    members = lax.axis_size("dp")
    factor = 1.0 / math.sqrt(rows * members)
    weight_full = lax.all_gather(weight, "dp", axis=0, tiled=True)
    output = jnp.dot(hidden, weight_full, preferred_element_type=jnp.float32)
    error = (output - target.astype(jnp.float32)).astype(jnp.bfloat16)
    product = lax.dot_general(
        hidden, error, (((0,), (0,)), ((), ())), preferred_element_type=jnp.float32
    )
    shard = lax.psum_scatter(
        (product * factor).astype(jnp.bfloat16), "dp", scatter_dimension=0, tiled=True
    ).astype(jnp.float32)
    hidden_grad = lax.dot_general(
        error, weight_full, (((1,), (1,)), ((), ())), preferred_element_type=jnp.float32
    ).astype(jnp.bfloat16)
    levels = lax.axis_size("grp").bit_length() - 1
    for level in range(levels):
        other = partner(shard.astype(jnp.bfloat16), "grp", level).astype(shard.dtype)
        own_sq, other_sq, cross = lax.psum(
            (jnp.sum(shard * shard), jnp.sum(other * other), jnp.sum(shard * other)), "dp"
        )
        coef_own, coef_other = coefficients(own_sq, other_sq, cross)
        shard = coef_own * shard + coef_other * other
    columns = shard.shape[1] // lax.axis_size("grp")
    mine = lax.dynamic_slice_in_dim(shard, lax.axis_index("grp") * columns, columns, 1)
    return (hidden_grad, mine)


def solution(mesh):
    in_specs = (P(("grp", "dp"), None), P("dp", None), P(("grp", "dp"), None))
    out_specs = (P(("grp", "dp"), None), P("dp", "grp"))
    return jax.shard_map(shards, mesh=mesh, in_specs=in_specs, out_specs=out_specs, check_vma=False)
```

profile of v0, /device:TPU:0, one launch (start us, length us, event | category | flops | bytes accessed | tf_op | source)
XLA Modules:
  0.0 175.9 jit_solution(18087885401114173631)
XLA Ops:
  7.2 0.0 copy-start
  7.2 0.0 all-gather.2.cloned.1.call-start
  7.2 0.7 all-gather.2.cloned.1.call-update
  7.9 0.0 reduce-scatter.4.cloned.1.call-start
  8.0 42.6 %all-gather.2.cloned.1.call-done = bf16[768,2048]{1,0:T(8,128)(2,1)} async-done(((bf16[96,2048]{1,0:T(8,128)(2,1)}), bf16[768,2048]{1,0:T(8,128)(2,1)}) %all-gather.2.cloned.1.call-update) | async-done | bytes 3145744 | tf_op jit(solution)/shard_map/all_gather | solution.py:24
  50.6 0.0 copy-done
  50.6 4.3 %subtract_convert_fusion = bf16[512,2048]{1,0:T(8,128)(2,1)S(1)} fusion(bf16[512,2048]{1,0:T(8,128)(2,1)} %param.5, bf16[512,768]{1,0:T(8,128)(2,1)S(1)} %copy-done, bf16[768,2048]{1,0:T(8,128)(2,1)} %all-gather.2.cloned.1.call-done), kind=kOutput, calls=%fused_computation.1 | convolution fusion | flops 1613758464 | bytes 8126464 | tf_op jit(solution)/shard_map/dot_general | solution.py:25
  54.9 0.0 copy-start.1
  55.0 1.3 copy-done.1
  56.3 3.6 %fusion = bf16[768,2048]{0,1:T(8,128)(2,1)} fusion(bf16[512,2048]{1,0:T(8,128)(2,1)S(1)} %subtract_convert_fusion, bf16[512,768]{1,0:T(8,128)(2,1)S(1)} %copy-done), kind=kOutput, calls=%fused_computation.2 | convolution fusion | flops 1613758464 | bytes 6029312 | tf_op jit(solution)/shard_map/dot_general | solution.py:27
  59.8 4.7 %copy.7 = bf16[768,2048]{1,0:T(8,128)(2,1)} copy(bf16[768,2048]{0,1:T(8,128)(2,1)} %fusion) | data formatting | bytes 6291456
  64.5 0.0 reduce-scatter.4.cloned.1.call-update
  64.6 39.4 %reduce-scatter.4.cloned.1.call-done = bf16[96,2048]{1,0:T(8,128)(2,1)} async-done(((bf16[768,2048]{1,0:T(8,128)(2,1)}), bf16[96,2048]{1,0:T(8,128)(2,1)}) %reduce-scatter.4.cloned.1.call-update) | async-done | bytes 393232
  104.0 1.3 copy.8
  105.3 1.5 collective-permute-start
  106.8 9.9 %collective-permute-done = bf16[96,2048]{0,1:T(8,128)(2,1)S(1)} collective-permute-done((bf16[96,2048]{0,1:T(8,128)(2,1)S(1)}, bf16[96,2048]{0,1:T(8,128)(2,1)S(1)}, u32[]{:S(2)}, u32[]{:S(2)}) %collective-permute-start) | collective-permute-done | bytes 393248 | tf_op jit(solution)/shard_map/ppermute | solution.py:12
  116.7 1.1 fusion.1
  117.8 17.3 %all-reduce.1 = (f32[]{:T(128)}, f32[]{:T(128)}, f32[]{:T(128)}) all-reduce(f32[]{:T(128)} %get-tuple-element.10, f32[]{:T(128)} %get-tuple-element.11, f32[]{:T(128)} %get-tuple-element.9), channel_id=1, replica_groups=mesh['grp'=4,'dp'=8] {'dp'}, use_global_device_ids=true, to_apply=%region_2.0 | all-reduce | flops 3 | bytes 24 | tf_op jit(solution)/shard_map/psum | solution.py:39
  137.7 0.2 fusion.6
  137.9 1.1 collective-permute-start.1
  139.0 5.2 %convolution_convert_fusion = bf16[512,768]{1,0:T(8,128)(2,1)} fusion(bf16[512,2048]{1,0:T(8,128)(2,1)} %copy-done.1, bf16[768,2048]{1,0:T(8,128)(2,1)} %all-gather.2.cloned.1.call-done), kind=kOutput, calls=%fused_computation.8 | convolution fusion | flops 1611005952 | bytes 6029312 | tf_op jit(solution)/shard_map/dot_general | solution.py:33
  144.2 4.4 %collective-permute-done.1 = bf16[96,2048]{0,1:T(8,128)(2,1)S(1)} collective-permute-done((bf16[96,2048]{0,1:T(8,128)(2,1)S(1)}, bf16[96,2048]{0,1:T(8,128)(2,1)S(1)}, u32[]{:S(2)}, u32[]{:S(2)}) %collective-permute-start.1) | collective-permute-done | bytes 393248 | tf_op jit(solution)/shard_map/ppermute | solution.py:12
  148.6 1.1 multiply_reduce_fusion.1
  149.7 15.9 %all-reduce = (f32[]{:T(128)}, f32[]{:T(128)}, f32[]{:T(128)}) all-reduce(f32[]{:T(128)} %get-tuple-element.7, f32[]{:T(128)} %get-tuple-element.8, f32[]{:T(128)} %get-tuple-element.6), channel_id=1, replica_groups=mesh['grp'=4,'dp'=8] {'dp'}, use_global_device_ids=true, to_apply=%region_8.0 | all-reduce | flops 3 | bytes 24 | tf_op jit(solution)/shard_map/psum | solution.py:39
  168.1 0.1 convert_element_type.36
  168.2 0.1 fusion.5
  168.2 0.8 copy.6
Async XLA Ops:
  7.2 43.4 %copy-start = (bf16[512,768]{1,0:T(8,128)(2,1)S(1)}, bf16[512,768]{1,0:T(8,128)(2,1)}, u32[]{:S(2)}) copy-start(bf16[512,768]{1,0:T(8,128)(2,1)} %param.3) | copy-start | bytes 2359300
  7.2 43.4 %all-gather.2.cloned.1.call-start = ((), (), s32[]{:S(2)}) async-start(), calls=%async_computation.1 | async-start | bytes 3538944 | tf_op jit(solution)/shard_map/all_gather | solution.py:24
  7.9 96.1 %reduce-scatter.4.cloned.1.call-start = ((), (), s32[]{:S(2)}) async-start(), calls=%async_computation.2 | async-start | bytes 3538944
  54.9 1.3 copy-start.1
  105.3 11.4 %collective-permute-start = (bf16[96,2048]{0,1:T(8,128)(2,1)S(1)}, bf16[96,2048]{0,1:T(8,128)(2,1)S(1)}, u32[]{:S(2)}, u32[]{:S(2)}) collective-permute-start(bf16[96,2048]{0,1:T(8,128)(2,1)S(1)} %copy.8), channel_id=1, source_target_pairs={{0,8},{8,0},{16,24},{24,16},{1,9},{9,1},{17,25},{25,17},{2,10},{10... | collective-permute-start | bytes 1179656 | tf_op jit(solution)/shard_map/ppermute | solution.py:12
  137.9 10.7 %collective-permute-start.1 = (bf16[96,2048]{0,1:T(8,128)(2,1)S(1)}, bf16[96,2048]{0,1:T(8,128)(2,1)S(1)}, u32[]{:S(2)}, u32[]{:S(2)}) collective-permute-start(bf16[96,2048]{0,1:T(8,128)(2,1)S(1)} %get-tuple-element.18), channel_id=1, source_target_pairs={{0,16},{8,24},{16,0},{24,8},{1,17},{9,25},{17,1},{25,9},{2,18},{10... | collective-permute-start | bytes 1179656 | tf_op jit(solution)/shard_map/ppermute | solution.py:12
Sparse Core Ops, SparseCore 0:
  9.6 40.9 all-gather.1
  64.7 39.2 reduce-scatter.3
where the time goes:
time: 176 us
  waiting for transfers between devices  97 us (55%)
  blocking collectives  33.2 us (19%)
  between operations  19.2 us (11%)
  matrix products  13.1 us (7%)
  local copies, waits for them, and re-layouts  8.09 us (5%)
  starting transfers between devices  2.68 us (2%)
  other arithmetic  2.5 us (1%)
    all_gather x1, waiting for transfers between devices, shards(): weight_full = lax.all_gather(weight, 'dp', axis=0, tiled=True)  42.6 us
    unnamed x3, waiting for transfers between devices  40.1 us
    psum x2, blocking collectives, shards(): lax.psum((jnp.sum(shard * shard), jnp.sum(other * other), jnp.sum(shard *...  33.2 us
    ppermute x2, waiting for transfers between devices, partner(): return lax.ppermute(value, axis, pairs)  14.3 us
    unnamed x7, local copies, waits for them, and re-layouts  8.09 us
    dot_general x1, matrix products, shards(): lax.dot_general(error, weight_full, (((1,), (1,)), ((), ())), preferred_e...  5.23 us
    dot_general x1, matrix products, shards(): output = jnp.dot(hidden, weight_full, preferred_element_type=jnp.float32)  4.34 us
    dot_general x1, matrix products, shards(): lax.dot_general(hidden, error, (((0,), (0,)), ((), ())), preferred_elemen...  3.57 us
  transfers between devices with their start and end apart: 4, of which 4 were waited for; matrix products, arithmetic and copies ran while one was open for 3% of the time, Pallas kernels for 0%

commit v1 on v0

--- a/solution.py
+++ b/solution.py
@@ -1,9 +1,15 @@
+import functools
 import math
 
 import jax
 import jax.numpy as jnp
 from jax import lax
+from jax.experimental import pallas as pl
+from jax.experimental.pallas import tpu as pltpu
 from jax.sharding import PartitionSpec as P
+
+CORES = 2
+EPS = 1e-06
 
 
 def partner(value, axis, stride):
@@ -13,11 +19,416 @@
 
 
 def coefficients(own_sq, other_sq, cross):
-    eps = 1e-06
-    return (1.0 - cross / (2.0 * (own_sq + eps)), 1.0 - cross / (2.0 * (other_sq + eps)))
-
-
-def shards(hidden, weight, target):
+    return (1.0 - cross / (2.0 * (own_sq + EPS)), 1.0 - cross / (2.0 * (other_sq + EPS)))
+
+
+def flip(value, other, size):
+    result, bit = 0, 1
+    while bit < size:
+        result = result + ((value // bit + other // bit) % 2) * bit
+        bit *= 2
+    return result
+
+
+def group_coefficients(gram, groups):
+    def inner(left, right):
+        total = 0.0
+        for i, a in left.items():
+            for j, b in right.items():
+                total = total + a * b * gram[min(i, j), max(i, j)]
+        return total
+
+    vectors = [{i: 1.0} for i in range(groups)]
+    while len(vectors) > 1:
+        merged = []
+        for first, second in zip(vectors[0::2], vectors[1::2]):
+            own_sq = jnp.maximum(inner(first, first), 0.0)
+            other_sq = jnp.maximum(inner(second, second), 0.0)
+            coef_own, coef_other = coefficients(own_sq, other_sq, inner(first, second))
+            both = {i: coef_own * a for i, a in first.items()}
+            both.update({i: coef_other * b for i, b in second.items()})
+            merged.append(both)
+        vectors = merged
+    return vectors[0]
+
+
+def kernel(
+    groups,
+    members,
+    factor,
+    hid_ref,
+    wsh_ref,
+    tgt_ref,
+    hg_ref,
+    comb_ref,
+    hid_t,
+    w_all,
+    term,
+    pair,
+    hop_in,
+    hop_out,
+    v_out,
+    gath,
+    gram_all,
+    gram_far,
+    gram_sum,
+    c_out,
+    c_in,
+    acc,
+    zs,
+    zr,
+    xs,
+    xr,
+    ss,
+    sr,
+    s2,
+    r2,
+    hs,
+    hr,
+    vs,
+    vr,
+    gs,
+    gr,
+    cs,
+    cr,
+):
+    depth = members // CORES
+    half = depth // 2
+    rows, width = wsh_ref.shape
+    cols = width // groups
+    ff = rows * members
+    g = lax.axis_index("grp")
+    d = lax.axis_index("dp")
+    z = d // CORES
+    c = d % CORES
+    sib = 1 - c
+
+    def copy(src, dst, send, recv, grp, dp):
+        return pltpu.make_async_remote_copy(
+            src_ref=src,
+            dst_ref=dst,
+            send_sem=send,
+            recv_sem=recv,
+            device_id=(grp, dp),
+            device_id_type=pl.DeviceIdType.MESH,
+        )
+
+    def col(m):
+        return pl.ds(pl.multiple_of(flip(g, m, groups) * cols, 128), cols)
+
+    barrier = pltpu.get_barrier_semaphore()
+    peers = [(g, flip(z, k, depth) * CORES + c) for k in range(1, depth)]
+    peers += [(flip(g, m, groups), d) for m in range(1, groups)]
+    peers += [(flip(g, m, groups), z * CORES + sib) for m in range(groups)]
+    for grp, dp in peers:
+        pl.semaphore_signal(
+            barrier, inc=1, device_id=(grp, dp), device_id_type=pl.DeviceIdType.MESH
+        )
+    pl.semaphore_wait(barrier, len(peers))
+
+    def z_copy(k):
+        return copy(
+            wsh_ref.at[:, col(0)],
+            w_all.at[0, d],
+            zs.at[k],
+            zr.at[k],
+            g,
+            flip(z, k, depth) * CORES + c,
+        )
+
+    def own_copy(m):
+        return copy(
+            wsh_ref.at[:, col(m)], w_all.at[m, d], ss.at[m, 0], sr.at[m, 0], g, z * CORES + sib
+        )
+
+    def x_copy(m, k):
+        row = flip(z, k, depth) * CORES + c
+        return copy(
+            w_all.at[0, row], w_all.at[m, row], xs.at[m, k], xr.at[m, k], flip(g, m, groups), d
+        )
+
+    def s_copy(m, k):
+        row = flip(z, k, depth) * CORES + c
+        return copy(
+            w_all.at[m, row], w_all.at[m, row], ss.at[m, k], sr.at[m, k], g, z * CORES + sib
+        )
+
+    for k in range(1, depth):
+        z_copy(k).start()
+    for m in range(groups):
+        own_copy(m).start()
+    for m in range(groups):
+        w_all[m, d] = wsh_ref[:, col(m)]
+    hid_t[...] = hid_ref[...].T
+
+    for k in range(1, depth):
+        z_copy(k).wait_recv()
+        s_copy(0, k).start()
+        for m in range(1, groups):
+            x_copy(m, k).start()
+
+    def pair_copy(s):
+        return copy(
+            term.at[s, sib], pair.at[s], s2.at[s], r2.at[s], g, z * CORES + sib
+        )
+
+    def hop_copy(s, way, j):
+        target = z - 1 if way == 0 else z + 1
+        return copy(
+            hop_out.at[s, way, j],
+            hop_in.at[s, way, j],
+            hs.at[s, way, j],
+            hr.at[s, way, j],
+            g,
+            target * CORES + c,
+        )
+
+    def v_copy(s, j):
+        return copy(
+            v_out.at[s, j], gath.at[g, j], vs.at[s, j], vr.at[s, j], flip(g, s, groups), d
+        )
+
+    def chip_sum(s, block):
+        return term[s, c, block].astype(jnp.float32) + pair[s, block].astype(jnp.float32)
+
+    def process(t):
+        for way in range(2):
+            place = depth - 1 - z if way == 0 else z
+            s = t - place
+            inside = (s >= 0) & (s < groups)
+
+            @pl.when(inside & (place == 0))
+            def _():
+                for j in range(half):
+                    hop_out[s, way, j] = chip_sum(s, way * half + j).astype(jnp.bfloat16)
+                    hop_copy(s, way, j).start()
+
+            @pl.when(inside & (place > 0) & (place < depth - 1))
+            def _():
+                for j in range(half):
+                    hop_copy(s, way, j).wait_recv()
+                    total = chip_sum(s, way * half + j) + hop_in[s, way, j].astype(jnp.float32)
+                    hop_out[s, way, j] = total.astype(jnp.bfloat16)
+                    hop_copy(s, way, j).start()
+
+            @pl.when(inside & (place == depth - 1))
+            def _():
+                for j in range(half):
+                    hop_copy(s, way, j).wait_recv()
+                    total = chip_sum(s, way * half + j) + hop_in[s, way, j].astype(jnp.float32)
+                    final = total.astype(jnp.bfloat16)
+
+                    @pl.when(s == 0)
+                    def _():
+                        gath[g, j] = final
+
+                    @pl.when(s > 0)
+                    def _():
+                        v_out[s, j] = final
+                        v_copy(s, j).start()
+
+    def slot(m, carry):
+        @pl.when(m > 0)
+        def _():
+            for k in range(1, depth):
+                x_copy(m, k).wait_recv()
+                s_copy(m, k).start()
+
+        for k in range(depth):
+            s_copy(m, k).wait_recv()
+        weight = w_all[m].reshape(ff, cols)
+        output = jnp.dot(hid_ref[...], weight, preferred_element_type=jnp.float32)
+        error = (output - tgt_ref[:, col(m)].astype(jnp.float32)).astype(jnp.bfloat16)
+        product = jnp.dot(hid_t[...], error, preferred_element_type=jnp.float32)
+        product = (product * factor).astype(jnp.bfloat16)
+        for i in range(members):
+            term[m, i % CORES, i // CORES] = product[i * rows : (i + 1) * rows]
+        pair_copy(m).start()
+        grad = lax.dot_general(
+            error, weight, (((1,), (1,)), ((), ())), preferred_element_type=jnp.float32
+        )
+
+        @pl.when(m == 0)
+        def _():
+            acc[...] = grad
+
+        @pl.when(m > 0)
+        def _():
+            acc[...] += grad
+
+        pair_copy(m).wait_recv()
+        process(m)
+        return carry
+
+    lax.fori_loop(0, groups, slot, 0)
+    hg_ref[...] = acc[...].astype(jnp.bfloat16)
+
+    def tail(t, carry):
+        process(t)
+        return carry
+
+    lax.fori_loop(groups, groups + depth - 1, tail, 0)
+
+    is_end = (z == 0) | (z == depth - 1)
+    pairs = [(i, j) for i in range(groups) for j in range(i, groups)]
+    near = [(m, e) for m in range(groups) for e in range(CORES) if m + e > 0]
+    far = (depth - 1 - z) * CORES + c
+
+    def near_copy(n):
+        m, e = near[n]
+        core = c if e == 0 else sib
+        return copy(
+            gram_sum.at[0],
+            gram_all.at[n],
+            gs.at[n],
+            gr.at[n],
+            flip(g, m, groups),
+            z * CORES + core,
+        )
+
+    def far_copy():
+        return copy(gram_sum.at[1], gram_far, gs.at[len(near)], gr.at[len(near)], g, far)
+
+    def c_copy(j, target):
+        return copy(c_out.at[j], c_in, cs.at[j], cr.at[0], g, target * CORES + c)
+
+    @pl.when(is_end)
+    def _():
+        for s in range(1, groups):
+            for j in range(half):
+                v_copy(s, j).wait_recv()
+        vecs = [gath[i].reshape(half * rows, cols).astype(jnp.float32) for i in range(groups)]
+        lines = []
+        for i, j in pairs:
+            line = jnp.sum(vecs[i] * vecs[j], axis=0, keepdims=True)
+            lines.append(sum(line[:, n * 128 : (n + 1) * 128] for n in range(cols // 128)))
+        pad = gram_sum.shape[1] - len(lines)
+        lines.append(jnp.zeros((pad, 128), jnp.float32))
+        mine = jnp.concatenate(lines, axis=0)
+        gram_sum[0] = mine
+        for n in range(len(near)):
+            near_copy(n).start()
+        for n in range(len(near)):
+            near_copy(n).wait_recv()
+        mine = mine + jnp.sum(gram_all[...], axis=0)
+        gram_sum[1] = mine
+        far_copy().start()
+        far_copy().wait_recv()
+        total = jnp.sum(mine + gram_far[...], axis=1, keepdims=True)
+        gram = {ij: total[n : n + 1] for n, ij in enumerate(pairs)}
+        coef = group_coefficients(gram, groups)
+        for j in range(half):
+            mixed = sum(coef[i] * gath[i, j].astype(jnp.float32) for i in range(groups))
+            for way in range(2):
+                target = way * half + j
+
+                @pl.when(z == way * (depth - 1))
+                def _():
+                    if target == way * (depth - 1):
+                        comb_ref[...] = mixed
+                    else:
+                        c_out[j] = mixed.astype(jnp.bfloat16)
+                        c_copy(j, target).start()
+
+        for s in range(1, groups):
+            for j in range(half):
+                v_copy(s, j).wait_send()
+        for n in range(len(near)):
+            near_copy(n).wait_send()
+        far_copy().wait_send()
+        for j in range(half):
+            for way in range(2):
+                target = way * half + j
+                if target != way * (depth - 1):
+
+                    @pl.when(z == way * (depth - 1))
+                    def _():
+                        c_copy(j, target).wait_send()
+
+    @pl.when(jnp.logical_not(is_end))
+    def _():
+        c_copy(0, 0).wait_recv()
+        comb_ref[...] = c_in[...].astype(jnp.float32)
+
+    for k in range(1, depth):
+        z_copy(k).wait_send()
+        for m in range(1, groups):
+            x_copy(m, k).wait_send()
+    for m in range(groups):
+        pair_copy(m).wait_send()
+        for k in range(depth):
+            s_copy(m, k).wait_send()
+        for way in range(2):
+
+            @pl.when(z != way * (depth - 1))
+            def _():
+                for j in range(half):
+                    hop_copy(m, way, j).wait_send()
+
+
+def fused(hidden, weight, target):
+    groups = lax.axis_size("grp")
+    members = lax.axis_size("dp")
+    tokens, ff = hidden.shape
+    rows, width = weight.shape
+    cols = width // groups
+    depth = members // CORES
+    half = depth // 2
+    factor = 1.0 / math.sqrt(tokens * members)
+    bf16, f32 = jnp.bfloat16, jnp.float32
+    pads = -(-(groups * (groups + 1) // 2) // 8) * 8 + 8
+    near = groups * CORES - 1
+    vmem = pl.BlockSpec(memory_space=pltpu.VMEM)
+    dma = pltpu.SemaphoreType.DMA
+    block = (rows, cols)
+    scratch = [
+        pltpu.VMEM((ff, tokens), bf16),
+        pltpu.VMEM((groups, members) + block, bf16),
+        pltpu.VMEM((groups, CORES, depth) + block, bf16),
+        pltpu.VMEM((groups, depth) + block, bf16),
+        pltpu.VMEM((groups, 2, half) + block, bf16),
+        pltpu.VMEM((groups, 2, half) + block, bf16),
+        pltpu.VMEM((groups, half) + block, bf16),
+        pltpu.VMEM((groups, half) + block, bf16),
+        pltpu.VMEM((near, pads, 128), f32),
+        pltpu.VMEM((pads, 128), f32),
+        pltpu.VMEM((2, pads, 128), f32),
+        pltpu.VMEM((half,) + block, bf16),
+        pltpu.VMEM(block, bf16),
+        pltpu.VMEM((tokens, ff), f32),
+        dma((depth,)),
+        dma((depth,)),
+        dma((groups, depth)),
+        dma((groups, depth)),
+        dma((groups, depth)),
+        dma((groups, depth)),
+        dma((groups,)),
+        dma((groups,)),
+        dma((groups, 2, half)),
+        dma((groups, 2, half)),
+        dma((groups, half)),
+        dma((groups, half)),
+        dma((near + 1,)),
+        dma((near + 1,)),
+        dma((half,)),
+        dma((1,)),
+    ]
+    return pl.pallas_call(
+        functools.partial(kernel, groups, members, factor),
+        out_shape=(
+            jax.ShapeDtypeStruct((tokens, ff), bf16),
+            jax.ShapeDtypeStruct(block, f32),
+        ),
+        in_specs=[vmem] * 3,
+        out_specs=(vmem, vmem),
+        scratch_shapes=scratch,
+        compiler_params=pltpu.CompilerParams(
+            collective_id=0, has_side_effects=True, vmem_limit_bytes=56 * 2**20
+        ),
+    )(hidden, weight, target)
+
+
+def plain(hidden, weight, target):
     rows = hidden.shape[0]
     members = lax.axis_size("dp")
     factor = 1.0 / math.sqrt(rows * members)
@@ -46,6 +457,16 @@
     return (hidden_grad, mine)
 
 
+def shards(hidden, weight, target):
+    groups, members = lax.axis_size("grp"), lax.axis_size("dp")
+    rows, width = weight.shape
+    power = all(n & (n - 1) == 0 for n in (groups, members))
+    aligned = rows % 16 == 0 and width % (128 * groups) == 0
+    if power and aligned and members >= 2 * CORES and groups > 1:
+        return fused(hidden, weight, target)
+    return plain(hidden, weight, target)
+
+
 def solution(mesh):
     in_specs = (P(("grp", "dp"), None), P("dp", None), P(("grp", "dp"), None))
     out_specs = (P(("grp", "dp"), None), P("dp", "grp"))

time: 176 us -> 75.4 us (0.43)
  waiting for transfers between devices: 97 us -> 0 us
  Pallas kernels: 0 us -> 70.9 us
  blocking collectives: 33.2 us -> 0 us
  between operations: 19.2 us -> 0.64 us
  matrix products: 13.1 us -> 0 us
  local copies, waits for them, and re-layouts: 8.09 us -> 3.68 us
  starting transfers between devices: 2.68 us -> 0 us
  other arithmetic: 2.5 us -> 0 us
    pallas_call x0 -> x1, Pallas kernels: none -> 70.9 us  [fused(): pl.pallas_call(functools.partial(kernel, groups, members, factor), out_sh...]
    all_gather x1 -> x0, waiting for transfers between devices: 42.6 us -> none  [shards(): weight_full = lax.all_gather(weight, 'dp', axis=0, tiled=True)]
    unnamed x3 -> x0, waiting for transfers between devices: 40.1 us -> none
    psum x2 -> x0, blocking collectives: 33.2 us -> none  [shards(): lax.psum((jnp.sum(shard * shard), jnp.sum(other * other), jnp.sum(shard *...]
    ppermute x2 -> x0, waiting for transfers between devices: 14.3 us -> none  [partner(): return lax.ppermute(value, axis, pairs)]
    dot_general x3 -> x0, matrix products: 13.1 us -> none  [the longest x1 5.23 us: shards(): lax.dot_general(error, weight_full, (((1,), (1,)), ((), ())), preferred_e...]
    unnamed x7 -> x2, local copies, waits for them, and re-layouts: 8.09 us -> 3.68 us
    ppermute x2 -> x0, starting transfers between devices: 2.6 us -> none  [partner(): return lax.ppermute(value, axis, pairs)]
  transfers between devices with their start and end apart: 4 -> 0, of which waited for: 4 -> 0; matrix products, arithmetic and copies ran while one was open for 3% -> 0% of each run, Pallas kernels for 0% -> 0%
where the time goes in v1:
time: 75.4 us; the launch traced here: 75.2 us
  Pallas kernels  70.9 us (94%)
  local copies, waits for them, and re-layouts  3.68 us (5%)
    pallas_call x1, Pallas kernels, fused(): pl.pallas_call(functools.partial(kernel, groups, members, factor), out_sh...  70.9 us
    unnamed x2, local copies, waits for them, and re-layouts  3.68 us

profile of v1, /device:TPU:0, one launch (start us, length us, event | category | flops | bytes accessed | tf_op | source)
XLA Modules:
  0.0 75.2 jit_solution(13393934209739447290)
XLA Ops:
  0.6 70.9 %shard_map.50 = (bf16[512,768]{1,0:T(8,128)(2,1)}, f32[96,512]{1,0:T(8,128)}) custom-call(bf16[512,768]{1,0:T(8,128)(2,1)} %hid_ref.1, bf16[96,2048]{1,0:T(8,128)(2,1)} %wsh_ref.1, bf16[512,2048]{1,0:T(8,128)(2,1)} %tgt_ref.1), custom_call_target="tpu_custom_call" | custom-call | tf_op jit(solution)/shard_map/pallas_call | solution.py:416
  71.6 2.1 %copy.7 = bf16[512,768]{1,0:T(8,128)(2,1)} copy(bf16[512,768]{1,0:T(8,128)(2,1)} %get-tuple-element.4) | data formatting | bytes 1572864
  73.6 1.6 %copy.8 = f32[96,512]{1,0:T(8,128)} copy(f32[96,512]{1,0:T(8,128)} %get-tuple-element.5) | data formatting | bytes 393216

commit v2 on v1

v2 whole, which is shorter than its diff:
```python
import functools
import math

import jax
import jax.numpy as jnp
from jax import lax
from jax.experimental import pallas as pl
from jax.experimental.pallas import tpu as pltpu
from jax.sharding import PartitionSpec as P

CORES = 2
PARTS = 2
EPS = 1e-06


def partner(value, axis, stride):
    mask = 2**stride
    pairs = [(source, source ^ mask) for source in range(lax.axis_size(axis))]
    return lax.ppermute(value, axis, pairs)


def coefficients(own_sq, other_sq, cross):
    return (1.0 - cross / (2.0 * (own_sq + EPS)), 1.0 - cross / (2.0 * (other_sq + EPS)))


def flip(value, other, size):
    result, bit = 0, 1
    while bit < size:
        result = result + ((value // bit + other // bit) % 2) * bit
        bit *= 2
    return result


def group_coefficients(gram, groups):
    def inner(left, right):
        total = 0.0
        for i, a in left.items():
            for j, b in right.items():
                total = total + a * b * gram[min(i, j), max(i, j)]
        return total

    vectors = [{i: 1.0} for i in range(groups)]
    while len(vectors) > 1:
        merged = []
        for first, second in zip(vectors[0::2], vectors[1::2]):
            own_sq = jnp.maximum(inner(first, first), 0.0)
            other_sq = jnp.maximum(inner(second, second), 0.0)
            coef_own, coef_other = coefficients(own_sq, other_sq, inner(first, second))
            both = {i: coef_own * a for i, a in first.items()}
            both.update({i: coef_other * b for i, b in second.items()})
            merged.append(both)
        vectors = merged
    return vectors[0]


def kernel(
    groups,
    members,
    factor,
    hid_hbm,
    wsh_ref,
    tgt_hbm,
    hg_hbm,
    comb_ref,
    hid_ref,
    tgt_ref,
    hg_ref,
    hid_t,
    w_all,
    term,
    pair,
    hop_in,
    hop_out,
    v_out,
    gath,
    gram_all,
    gram_far,
    gram_sum,
    acc,
    zs,
    zr,
    xs,
    xr,
    ds,
    dr,
    ss,
    sr,
    s2,
    r2,
    hs,
    hr,
    vs,
    vr,
    gs,
    gr,
    ms,
    mr,
    fs,
    fr,
    local,
):
    depth = members // CORES
    half = depth // 2
    rows, width = wsh_ref.shape
    cols = width // groups
    ff = rows * members
    g = lax.axis_index("grp")
    d = lax.axis_index("dp")
    z = d // CORES
    c = d % CORES
    sib = 1 - c
    is_end = (z == 0) | (z == depth - 1)
    end = z // (depth - 1)
    held = end * (half - 1)

    def part(p):
        return pl.ds(p * (rows // PARTS), rows // PARTS)


    def copy(src, dst, send, recv, grp, dp):
        return pltpu.make_async_remote_copy(
            src_ref=src,
            dst_ref=dst,
            send_sem=send,
            recv_sem=recv,
            device_id=(grp, dp),
            device_id_type=pl.DeviceIdType.MESH,
        )

    def col(m):
        return pl.ds(pl.multiple_of(flip(g, m, groups) * cols, 128), cols)

    hid_load = pltpu.make_async_copy(hid_hbm, hid_ref, local.at[0])
    tgt_load = pltpu.make_async_copy(tgt_hbm, tgt_ref, local.at[1])
    hg_store = pltpu.make_async_copy(hg_ref, hg_hbm, local.at[2])

    def own_load(m):
        return pltpu.make_async_copy(wsh_ref.at[:, col(m)], w_all.at[m, d], local.at[3 + m])

    barrier = pltpu.get_barrier_semaphore()
    peers = [(g, flip(z, k, depth) * CORES + c) for k in range(1, depth)]
    peers += [(flip(g, m, groups), d) for m in range(1, groups)]
    peers += [(flip(g, m, groups), z * CORES + sib) for m in range(groups)]
    for grp, dp in peers:
        pl.semaphore_signal(
            barrier, inc=1, device_id=(grp, dp), device_id_type=pl.DeviceIdType.MESH
        )
    pl.semaphore_wait(barrier, len(peers))

    def z_copy(src, way, block):
        target = z - 1 if way == 0 else z + 1
        row = src * CORES + c
        return copy(
            block, w_all.at[0, row], zs.at[way, src], zr.at[src], g, target * CORES + c
        )

    def own_copy(m):
        return copy(
            wsh_ref.at[:, col(m)], w_all.at[m, d], ss.at[m, z], sr.at[m, z], g, z * CORES + sib
        )

    def x_copy(m, src):
        row = src * CORES + c
        return copy(
            w_all.at[0, row], w_all.at[m, row], xs.at[m, src], xr.at[m, src], flip(g, m, groups), d
        )

    def d_copy(side, src):
        side_rows = pl.ds(side * (rows // 2), rows // 2)
        row = src * CORES + c
        return copy(
            w_all.at[1 + side, row, side_rows],
            w_all.at[3, row, side_rows],
            ds.at[side, src],
            dr.at[side, src],
            flip(g, 2 - side, groups),
            d,
        )

    def s_copy(m, src):
        row = src * CORES + c
        return copy(
            w_all.at[m, row], w_all.at[m, row], ss.at[m, src], sr.at[m, src], g, z * CORES + sib
        )

    def at_distance(h, action):
        for way in range(2):
            src = z + h if way == 0 else z - h

            @pl.when((src >= 0) & (src < depth))
            def _():
                action(src, way)

    def sends_on(way):
        return z > 0 if way == 0 else z < depth - 1

    def line_step(src, way):
        z_copy(src, way, wsh_ref.at[:, col(0)]).wait_recv()

        @pl.when(sends_on(way))
        def _():
            z_copy(src, way, w_all.at[0, src * CORES + c]).start()

        x_copy(1, src).start()
        x_copy(2, src).start()
        s_copy(0, src).start()

    def cross_step(src, way):
        for m in (1, 2):
            x_copy(m, src).wait_recv()
            d_copy(m - 1, src).start()
            s_copy(m, src).start()

    def corner_step(src, way):
        for side in range(2):
            d_copy(side, src).wait_recv()
        s_copy(3, src).start()

    for way in range(2):

        @pl.when(sends_on(way))
        def _():
            z_copy(z, way, wsh_ref.at[:, col(0)]).start()

    for m in range(groups):
        own_copy(m).start()
    for m in range(groups):
        own_load(m).start()
    hid_load.start()
    tgt_load.start()
    hid_load.wait()
    hid_t[...] = hid_ref[...].T

    for h in range(1, depth):
        at_distance(h, line_step)
        if 1 <= h - 1 < depth - 2:
            at_distance(h - 1, cross_step)
    tgt_load.wait()
    for m in range(groups):
        own_load(m).wait()

    def pair_copy(s):
        return copy(
            term.at[s, sib], pair.at[s], s2.at[s], r2.at[s], g, z * CORES + sib
        )

    def hop_copy(s, way, j, p):
        target = z - 1 if way == 0 else z + 1
        return copy(
            hop_out.at[s, way, j, part(p)],
            hop_in.at[s, way, j, part(p)],
            hs.at[s, way, j, p],
            hr.at[s, way, j, p],
            g,
            target * CORES + c,
        )

    def v_copy(s, j, p):
        return copy(
            v_out.at[s, j, part(p)],
            gath.at[g, j, part(p)],
            vs.at[s, j, p],
            vr.at[s, j, p],
            flip(g, s, groups),
            d,
        )

    def m_copy(s, j):
        group = flip(g, s, groups)
        return copy(
            gath.at[group, j],
            gath.at[group, 0],
            ms.at[s, j],
            mr.at[s],
            g,
            (end * half + j) * CORES + c,
        )

    def pieces():
        return [(j, p) for j in range(half) for p in range(PARTS)]

    def to_middle(action):
        for j in range(half):

            @pl.when(j != held)
            def _():
                action(j)

    def forward(s):
        @pl.when(s > 0)
        def _():
            for j, p in pieces():
                v_copy(s, j, p).wait_recv()

        to_middle(lambda j: m_copy(s, j).start())

    def chip_sum(s, block, p):
        return term[s, c, block, part(p)].astype(jnp.float32) + pair[s, block, part(p)].astype(
            jnp.float32
        )

    def process(t):
        for way in range(2):
            place = depth - 1 - z if way == 0 else z
            s = t - place
            inside = (s >= 0) & (s < groups)

            @pl.when(inside & (place == 0))
            def _():
                for j, p in pieces():
                    mine = chip_sum(s, way * half + j, p)
                    hop_out[s, way, j, part(p)] = mine.astype(jnp.bfloat16)
                    hop_copy(s, way, j, p).start()

            @pl.when(inside & (place > 0) & (place < depth - 1))
            def _():
                for j, p in pieces():
                    mine = chip_sum(s, way * half + j, p)
                    hop_copy(s, way, j, p).wait_recv()
                    total = mine + hop_in[s, way, j, part(p)].astype(jnp.float32)
                    hop_out[s, way, j, part(p)] = total.astype(jnp.bfloat16)
                    hop_copy(s, way, j, p).start()

            @pl.when(inside & (place == depth - 1))
            def _():
                for j, p in pieces():
                    mine = chip_sum(s, way * half + j, p)
                    hop_copy(s, way, j, p).wait_recv()
                    total = mine + hop_in[s, way, j, part(p)].astype(jnp.float32)
                    final = total.astype(jnp.bfloat16)

                    @pl.when(s == 0)
                    def _():
                        gath[g, j, part(p)] = final

                    @pl.when(s > 0)
                    def _():
                        v_out[s, j, part(p)] = final
                        v_copy(s, j, p).start()

        s1 = t - depth

        @pl.when(is_end & (s1 >= 0) & (s1 < groups - 1))
        def _():
            forward(s1)

    def slot(m, carry):
        @pl.when(m == 1)
        def _():
            for h in range(max(1, depth - 2), depth):
                at_distance(h, cross_step)

        @pl.when(m == 2)
        def _():
            for h in range(1, depth):
                at_distance(h, corner_step)

        for k in range(depth):
            s_copy(m, k).wait_recv()
        weight = w_all[m].reshape(ff, cols)
        output = jnp.dot(hid_ref[...], weight, preferred_element_type=jnp.float32)
        error = (output - tgt_ref[:, col(m)].astype(jnp.float32)).astype(jnp.bfloat16)
        product = jnp.dot(hid_t[...], error, preferred_element_type=jnp.float32)
        product = (product * factor).astype(jnp.bfloat16)
        for i in range(members):
            term[m, i % CORES, i // CORES] = product[i * rows : (i + 1) * rows]
        pair_copy(m).start()
        grad = lax.dot_general(
            error, weight, (((1,), (1,)), ((), ())), preferred_element_type=jnp.float32
        )

        @pl.when(m == 0)
        def _():
            acc[...] = grad

        @pl.when(m > 0)
        def _():
            acc[...] += grad

        pair_copy(m).wait_recv()
        process(m)
        return carry

    lax.fori_loop(0, groups, slot, 0)
    hg_ref[...] = acc[...].astype(jnp.bfloat16)
    hg_store.start()

    def tail(t, carry):
        process(t)
        return carry

    lax.fori_loop(groups, groups + depth - 1, tail, 0)

    pairs = [(i, j) for i in range(groups) for j in range(i, groups)]
    near = [(m, e) for m in range(groups) for e in range(CORES) if m + e > 0]

    def near_copy(n):
        m, e = near[n]
        core = c if e == 0 else sib
        return copy(
            gram_sum,
            gram_all.at[n],
            gs.at[n],
            gr.at[n],
            flip(g, m, groups),
            z * CORES + core,
        )

    def far_copy(k, e):
        return copy(
            gram_far.at[e],
            gram_far.at[e],
            fs.at[k],
            fr.at[e],
            g,
            flip(z, k, depth) * CORES + c,
        )

    @pl.when(is_end)
    def _():
        forward(groups - 1)
        vecs = [gath[i].reshape(half * rows, cols).astype(jnp.float32) for i in range(groups)]
        lines = []
        for i, j in pairs:
            line = jnp.sum(vecs[i] * vecs[j], axis=0, keepdims=True)
            lines.append(sum(line[:, n * 128 : (n + 1) * 128] for n in range(cols // 128)))
        pad = gram_sum.shape[0] - len(lines)
        lines.append(jnp.zeros((pad, 128), jnp.float32))
        mine = jnp.concatenate(lines, axis=0)
        gram_sum[...] = mine
        for n in range(len(near)):
            near_copy(n).start()
        for n in range(len(near)):
            near_copy(n).wait_recv()
        gram_far[end] = mine + jnp.sum(gram_all[...], axis=0)
        for k in range(1, depth):
            far_copy(k, end).start()
        far_copy(1, 1 - end).wait_recv()

    @pl.when(jnp.logical_not(is_end))
    def _():
        for s in range(groups):
            m_copy(s, 0).wait_recv()
        for e in range(2):
            far_copy(1, e).wait_recv()

    total = jnp.sum(gram_far[0] + gram_far[1], axis=1, keepdims=True)
    gram = {ij: total[n : n + 1] for n, ij in enumerate(pairs)}
    coef = group_coefficients(gram, groups)
    comb_ref[...] = sum(coef[i] * gath[i, held].astype(jnp.float32) for i in range(groups))

    @pl.when(is_end)
    def _():
        for s in range(1, groups):
            for j, p in pieces():
                v_copy(s, j, p).wait_send()
        for s in range(groups):
            to_middle(lambda j: m_copy(s, j).wait_send())
        for n in range(len(near)):
            near_copy(n).wait_send()
        for k in range(1, depth):
            far_copy(k, end).wait_send()

    for way in range(2):
        for h in range(depth):
            src = z - h if way else z + h

            @pl.when(sends_on(way) & (src >= 0) & (src < depth))
            def _():
                z_copy(src, way, wsh_ref.at[:, col(0)]).wait_send()

    def cross_done(src, way):
        for m in (1, 2):
            x_copy(m, src).wait_send()
            d_copy(m - 1, src).wait_send()

    for h in range(1, depth):
        at_distance(h, cross_done)
    hg_store.wait()
    for m in range(groups):
        pair_copy(m).wait_send()
        for k in range(depth):
            s_copy(m, k).wait_send()
        for way in range(2):

            @pl.when(z != way * (depth - 1))
            def _():
                for j, p in pieces():
                    hop_copy(m, way, j, p).wait_send()


def fused(hidden, weight, target):
    groups = lax.axis_size("grp")
    members = lax.axis_size("dp")
    tokens, ff = hidden.shape
    rows, width = weight.shape
    cols = width // groups
    depth = members // CORES
    half = depth // 2
    factor = 1.0 / math.sqrt(tokens * members)
    bf16, f32 = jnp.bfloat16, jnp.float32
    pads = -(-(groups * (groups + 1) // 2) // 8) * 8 + 8
    near = groups * CORES - 1
    vmem = pl.BlockSpec(memory_space=pltpu.VMEM)
    hbm = pl.BlockSpec(memory_space=pltpu.HBM)
    dma = pltpu.SemaphoreType.DMA
    block = (rows, cols)
    scratch = [
        pltpu.VMEM((tokens, ff), bf16),
        pltpu.VMEM((tokens, width), bf16),
        pltpu.VMEM((tokens, ff), bf16),
        pltpu.VMEM((ff, tokens), bf16),
        pltpu.VMEM((groups, members) + block, bf16),
        pltpu.VMEM((groups, CORES, depth) + block, bf16),
        pltpu.VMEM((groups, depth) + block, bf16),
        pltpu.VMEM((groups, 2, half) + block, bf16),
        pltpu.VMEM((groups, 2, half) + block, bf16),
        pltpu.VMEM((groups, half) + block, bf16),
        pltpu.VMEM((groups, half) + block, bf16),
        pltpu.VMEM((near, pads, 128), f32),
        pltpu.VMEM((2, pads, 128), f32),
        pltpu.VMEM((pads, 128), f32),
        pltpu.VMEM((tokens, ff), f32),
        dma((2, depth)),
        dma((depth,)),
        dma((groups, depth)),
        dma((groups, depth)),
        dma((2, depth)),
        dma((2, depth)),
        dma((groups, depth)),
        dma((groups, depth)),
        dma((groups,)),
        dma((groups,)),
        dma((groups, 2, half, PARTS)),
        dma((groups, 2, half, PARTS)),
        dma((groups, half, PARTS)),
        dma((groups, half, PARTS)),
        dma((near,)),
        dma((near,)),
        dma((groups, half)),
        dma((groups,)),
        dma((depth,)),
        dma((2,)),
        dma((3 + groups,)),
    ]
    return pl.pallas_call(
        functools.partial(kernel, groups, members, factor),
        out_shape=(
            jax.ShapeDtypeStruct((tokens, ff), bf16),
            jax.ShapeDtypeStruct(block, f32),
        ),
        in_specs=[hbm] * 3,
        out_specs=(hbm, vmem),
        scratch_shapes=scratch,
        compiler_params=pltpu.CompilerParams(
            collective_id=0, has_side_effects=True, vmem_limit_bytes=56 * 2**20
        ),
    )(hidden, weight, target)


def plain(hidden, weight, target):
    rows = hidden.shape[0]
    members = lax.axis_size("dp")
    factor = 1.0 / math.sqrt(rows * members)
    weight_full = lax.all_gather(weight, "dp", axis=0, tiled=True)
    output = jnp.dot(hidden, weight_full, preferred_element_type=jnp.float32)
    error = (output - target.astype(jnp.float32)).astype(jnp.bfloat16)
    product = lax.dot_general(
        hidden, error, (((0,), (0,)), ((), ())), preferred_element_type=jnp.float32
    )
    shard = lax.psum_scatter(
        (product * factor).astype(jnp.bfloat16), "dp", scatter_dimension=0, tiled=True
    ).astype(jnp.float32)
    hidden_grad = lax.dot_general(
        error, weight_full, (((1,), (1,)), ((), ())), preferred_element_type=jnp.float32
    ).astype(jnp.bfloat16)
    levels = lax.axis_size("grp").bit_length() - 1
    for level in range(levels):
        other = partner(shard.astype(jnp.bfloat16), "grp", level).astype(shard.dtype)
        own_sq, other_sq, cross = lax.psum(
            (jnp.sum(shard * shard), jnp.sum(other * other), jnp.sum(shard * other)), "dp"
        )
        coef_own, coef_other = coefficients(own_sq, other_sq, cross)
        shard = coef_own * shard + coef_other * other
    columns = shard.shape[1] // lax.axis_size("grp")
    mine = lax.dynamic_slice_in_dim(shard, lax.axis_index("grp") * columns, columns, 1)
    return (hidden_grad, mine)


def shards(hidden, weight, target):
    groups, members = lax.axis_size("grp"), lax.axis_size("dp")
    rows, width = weight.shape
    power = all(n & (n - 1) == 0 for n in (groups, members))
    aligned = rows % (16 * PARTS) == 0 and width % (128 * groups) == 0
    if power and aligned and members >= 2 * CORES and groups == 4:
        return fused(hidden, weight, target)
    return plain(hidden, weight, target)


def solution(mesh):
    in_specs = (P(("grp", "dp"), None), P("dp", None), P(("grp", "dp"), None))
    out_specs = (P(("grp", "dp"), None), P("dp", "grp"))
    return jax.shard_map(shards, mesh=mesh, in_specs=in_specs, out_specs=out_specs, check_vma=False)
```

time: 75.4 us -> 67.7 us (0.90)
  Pallas kernels: 70.9 us -> 63.2 us
    pallas_call x1, Pallas kernels: 70.9 us -> 63.2 us  [fused(): pl.pallas_call(functools.partial(kernel, groups, members, factor), out_sh...]
where the time goes in v2:
time: 67.7 us; the launch traced here: 67.5 us
  Pallas kernels  63.2 us (93%)
  local copies, waits for them, and re-layouts  3.68 us (5%)
    pallas_call x1, Pallas kernels, fused(): pl.pallas_call(functools.partial(kernel, groups, members, factor), out_sh...  63.2 us
    unnamed x2, local copies, waits for them, and re-layouts  3.68 us

profile of v2, /device:TPU:0, one launch (start us, length us, event | category | flops | bytes accessed | tf_op | source)
XLA Modules:
  0.0 67.5 jit_solution(15506490293458856977)
XLA Ops:
  0.6 63.2 %shard_map.50 = (bf16[512,768]{1,0:T(8,128)(2,1)}, f32[96,512]{1,0:T(8,128)}) custom-call(bf16[512,768]{1,0:T(8,128)(2,1)} %hid_hbm.1, bf16[96,2048]{1,0:T(8,128)(2,1)} %wsh_ref.1, bf16[512,2048]{1,0:T(8,128)(2,1)} %tgt_hbm.1), custom_call_target="tpu_custom_call" | custom-call | tf_op jit(solution)/shard_map/pallas_call | solution.py:546
  63.8 2.1 %copy.7 = bf16[512,768]{1,0:T(8,128)(2,1)} copy(bf16[512,768]{1,0:T(8,128)(2,1)} %get-tuple-element.4) | data formatting | bytes 1572864
  65.9 1.6 %copy.8 = f32[96,512]{1,0:T(8,128)} copy(f32[96,512]{1,0:T(8,128)} %get-tuple-element.5) | data formatting | bytes 393216

commit v3 on v2

--- a/solution.py
+++ b/solution.py
@@ -489,6 +489,24 @@
                     hop_copy(m, way, j, p).wait_send()
 
 
+def put_out(hg_in, comb_in, hg_out, comb_out, hg_buf, comb_buf, sems):
+    loads = [
+        pltpu.make_async_copy(comb_in, comb_buf, sems.at[0]),
+        pltpu.make_async_copy(hg_in, hg_buf, sems.at[1]),
+    ]
+    stores = [
+        pltpu.make_async_copy(comb_buf, comb_out, sems.at[2]),
+        pltpu.make_async_copy(hg_buf, hg_out, sems.at[3]),
+    ]
+    for load in loads:
+        load.start()
+    for load, store in zip(loads, stores):
+        load.wait()
+        store.start()
+    for store in stores:
+        store.wait()
+
+
 def fused(hidden, weight, target):
     groups = lax.axis_size("grp")
     members = lax.axis_size("dp")
@@ -543,7 +561,7 @@
         dma((2,)),
         dma((3 + groups,)),
     ]
-    return pl.pallas_call(
+    results = pl.pallas_call(
         functools.partial(kernel, groups, members, factor),
         out_shape=(
             jax.ShapeDtypeStruct((tokens, ff), bf16),
@@ -556,6 +574,17 @@
             collective_id=0, has_side_effects=True, vmem_limit_bytes=56 * 2**20
         ),
     )(hidden, weight, target)
+    return pl.pallas_call(
+        put_out,
+        out_shape=tuple(jax.ShapeDtypeStruct(r.shape, r.dtype) for r in results),
+        in_specs=[hbm, hbm],
+        out_specs=(hbm, hbm),
+        scratch_shapes=[
+            pltpu.VMEM((tokens, ff), bf16),
+            pltpu.VMEM(block, f32),
+            dma((4,)),
+        ],
+    )(*results)
 
 
 def plain(hidden, weight, target):

time: 67.7 us -> 66.1 us (0.976)
  local copies, waits for them, and re-layouts: 3.68 us -> 0 us
  Pallas kernels: 63.2 us -> 65.3 us
    unnamed x2 -> x0, local copies, waits for them, and re-layouts: 3.68 us -> none
    pallas_call x0 -> x1, Pallas kernels: none -> 2.16 us  [fused(): pl.pallas_call(put_out, out_shape=tuple((jax.ShapeDtypeStruct(r.shape, r....]
where the time goes in v3:
time: 66.1 us; the launch traced here: 66 us
  Pallas kernels  65.3 us (99%)
    pallas_call x1, Pallas kernels, fused(): pl.pallas_call(functools.partial(kernel, groups, members, factor), out_sh...  63.2 us
    pallas_call x1, Pallas kernels, fused(): pl.pallas_call(put_out, out_shape=tuple((jax.ShapeDtypeStruct(r.shape, r....  2.16 us

profile of v3, /device:TPU:0, one launch (start us, length us, event | category | flops | bytes accessed | tf_op | source)
XLA Modules:
  0.0 66.0 jit_solution(13184108886940199130)
XLA Ops:
  0.6 63.2 %shard_map.50 = (bf16[512,768]{1,0:T(8,128)(2,1)}, f32[96,512]{1,0:T(8,128)}) custom-call(bf16[512,768]{1,0:T(8,128)(2,1)} %hid_hbm.1, bf16[96,2048]{1,0:T(8,128)(2,1)} %wsh_ref.1, bf16[512,2048]{1,0:T(8,128)(2,1)} %tgt_hbm.1), custom_call_target="tpu_custom_call" | custom-call | tf_op jit(solution)/shard_map/pallas_call | solution.py:564
  63.8 2.2 %shard_map.51 = (bf16[512,768]{1,0:T(8,128)(2,1)}, f32[96,512]{1,0:T(8,128)}) custom-call(bf16[512,768]{1,0:T(8,128)(2,1)} %get-tuple-element.4.hg_in, f32[96,512]{1,0:T(8,128)} %get-tuple-element.5.comb_in), custom_call_target="tpu_custom_call" | custom-call | tf_op jit(solution)/shard_map/pallas_call | solution.py:577
